TPU v7x, 32 devices: a whole 2x2x4 slice. The times are simulated.
32 devices in a mesh: fsdp: 4 (over y, x), ctx: 4 (over z), tp: 2 (over core).
Axes of the slice: x: 2, y: 2, z: 4, core: 2. Of those that a mesh axis runs over, the one named last changes fastest.
Arguments:
- tokens: bfloat16 [8, 1024, 2048], P('fsdp', 'ctx'), may hold values from -6 to 6
- cotangent: bfloat16 [8, 1024, 2048], P('fsdp', 'ctx'), may hold values from -6 to 6
- prefix_len: int32 [8], P('fsdp'), may hold values from 102 to 512
- group_order: int32 [8], replicated, may hold values from 0 to 7, each once
- ln_gain: bfloat16 [2048], replicated, may hold values from 0.25 to 1.75
- ln_bias: bfloat16 [2048], replicated, may hold values from -4 to 4
- query_weight: bfloat16 [2048, 2048], P('fsdp', 'tp'), may hold values from -0.125 to 0.125
- query_bias: bfloat16 [2048], P('tp'), may hold values from -4 to 4
- key_weight: bfloat16 [2048, 2048], P('fsdp', 'tp'), may hold values from -0.125 to 0.125
- key_bias: bfloat16 [2048], P('tp'), may hold values from -4 to 4
- value_weight: bfloat16 [2048, 2048], P('fsdp', 'tp'), may hold values from -0.125 to 0.125
- value_bias: bfloat16 [2048], P('tp'), may hold values from -4 to 4
- out_weight: bfloat16 [2048, 2048], P('fsdp', 'tp'), may hold values from -1 to 1
- out_bias: bfloat16 [2048], replicated, may hold values from -4 to 4
- up_weight: bfloat16 [2048, 8192], P('fsdp', 'tp'), may hold values from -0.125 to 0.125
- up_bias: bfloat16 [8192], P('tp'), may hold values from -4 to 4
- down_weight: bfloat16 [2048, 8192], P('fsdp', 'tp'), may hold values from -0.0625 to 0.0625
- down_bias: bfloat16 [2048], replicated, may hold values from -4 to 4
Outputs:
- output: bfloat16 [8, 1024, 2048], P('fsdp', 'ctx')
- input_grad: bfloat16 [8, 1024, 2048], P('fsdp', 'ctx')
- ln_gain_grad: float32 [2048], replicated
- ln_bias_grad: float32 [2048], replicated
- query_weight_grad: float32 [2048, 2048], P('fsdp', 'tp')
- query_bias_grad: float32 [2048], P('tp')
- key_weight_grad: float32 [2048, 2048], P('fsdp', 'tp')
- key_bias_grad: float32 [2048], P('tp')
- value_weight_grad: float32 [2048, 2048], P('fsdp', 'tp')
- value_bias_grad: float32 [2048], P('tp')
- out_weight_grad: float32 [2048, 2048], P('fsdp', 'tp')
- up_weight_grad: float32 [2048, 8192], P('fsdp', 'tp')
- up_bias_grad: float32 [8192], P('tp')
- down_weight_grad: float32 [2048, 8192], P('fsdp', 'tp')
- out_biases_grad: float32 [2048], replicated
Inputs may be any that keep to these rules, and one draw needn't show every extreme that they name: Each number of 0 to 7 appears once; storage rows k * 128 to k * 128 + 127 of every sequence hold positions group_order[k] * 128 onwards.
All inputs are finite; a program needn't handle non-finite values.
Results may differ from a plain program's by a relative error of at most 0.012.
Values may be sent and summed in bfloat16 or wider, within the bound.
No kernel may reach another device: no remote copies, remote signals or barrier semaphores. Data moves between devices by JAX's collectives and lax.ppermute only.
A program may use at most 448 MiB of HBM per device.

v0:
```python
import jax
import jax.numpy as jnp
from jax import lax
from jax.sharding import PartitionSpec as P

HD = 64
ROT = 32
SEQ_LEN = 1024
masked_fill = -1e30
norm_eps = 1e-05


def positions(group_order, row_start, row_count, group_len):
    row_index = row_start + jnp.arange(row_count, dtype=jnp.int32)
    slot_index = row_index // group_len
    offset = row_index - slot_index * group_len
    matches = slot_index[:, None] == jnp.arange(group_order.shape[0], dtype=jnp.int32)[None, :]
    anchor = jnp.sum(jnp.where(matches, group_order[None, :], 0), axis=1)
    return anchor * group_len + offset


def rotary_tables(places):
    half_rot = ROT // 2
    frequency = jnp.power(10000.0, -2.0 * jnp.arange(half_rot, dtype=jnp.float32) / ROT)
    angles = places.astype(jnp.float32)[:, None] * frequency[None, :]
    return (jnp.cos(angles), jnp.sin(angles))


def rotate(tensor, cosine, sine_vals):
    half_rot = cosine.shape[-1]
    front_part = tensor[..., :half_rot]
    back_part = tensor[..., half_rot : 2 * half_rot]
    rest_part = tensor[..., 2 * half_rot :]
    cosine_rows = cosine[:, None, :]
    sine_rows = sine_vals[:, None, :]
    return jnp.concatenate(
        [
            front_part * cosine_rows - back_part * sine_rows,
            back_part * cosine_rows + front_part * sine_rows,
            rest_part,
        ],
        axis=-1,
    )


def gelu_tanh(values_in):
    return jax.nn.gelu(values_in, approximate=True)


def local(
    tokens,
    cotangent,
    prefix_len,
    group_order,
    ln_gain,
    ln_bias,
    query_weight,
    query_bias,
    key_weight,
    key_bias,
    value_weight,
    value_bias,
    out_weight,
    out_bias,
    up_weight,
    up_bias,
    down_weight,
    down_bias,
):
    seq_count, local_rows, model_width = tokens.shape
    token_count = seq_count * local_rows
    inner_width = query_weight.shape[1]
    local_heads = inner_width // HD
    hidden_units = up_weight.shape[1]
    group_len = SEQ_LEN // group_order.shape[0]
    score_scale = HD ** (-0.5)
    own_place = positions(group_order, lax.axis_index("ctx") * local_rows, local_rows, group_len)
    key_place = positions(group_order, 0, SEQ_LEN, group_len)
    cosine, sine_vals = rotary_tables(own_place)
    allowed = (key_place[None, None, None, :] <= own_place[None, None, :, None]) | (
        key_place[None, None, None, :] < prefix_len[:, None, None, None]
    )
    gathered = (
        lax.all_gather(query_weight, "fsdp", axis=0, tiled=True),
        lax.all_gather(key_weight, "fsdp", axis=0, tiled=True),
        lax.all_gather(value_weight, "fsdp", axis=0, tiled=True),
        lax.all_gather(out_weight, "fsdp", axis=0, tiled=True),
        lax.all_gather(up_weight, "fsdp", axis=0, tiled=True),
        lax.all_gather(down_weight, "fsdp", axis=0, tiled=True),
    )
    w_query, w_key, w_value, w_out, w_up, w_down = gathered
    inputs = tokens.reshape(token_count, model_width).astype(jnp.float32)
    centre = jnp.mean(inputs, axis=-1, keepdims=True)
    centred = inputs - centre
    inv_std = lax.rsqrt(jnp.mean(centred * centred, axis=-1, keepdims=True) + norm_eps)
    normed = centred * inv_std
    norm_gain = ln_gain.astype(jnp.float32)
    hidden = (normed * norm_gain + ln_bias.astype(jnp.float32)).astype(jnp.bfloat16)

    def project(weight, bias_vec):
        return jnp.dot(hidden, weight, preferred_element_type=jnp.float32) + bias_vec.astype(
            jnp.float32
        )

    query_rot = rotate(
        project(w_query, query_bias).reshape(seq_count, local_rows, local_heads, HD),
        cosine,
        sine_vals,
    ).astype(jnp.bfloat16)
    key_rot = (
        rotate(
            project(w_key, key_bias).reshape(seq_count, local_rows, local_heads, HD),
            cosine,
            sine_vals,
        )
        .astype(jnp.bfloat16)
        .reshape(seq_count, local_rows, inner_width)
    )
    value_rows = (
        project(w_value, value_bias)
        .astype(jnp.bfloat16)
        .reshape(seq_count, local_rows, inner_width)
    )
    keys_all, values_all = (
        lax.all_gather(key_rot, "ctx", axis=1, tiled=True),
        lax.all_gather(value_rows, "ctx", axis=1, tiled=True),
    )

    def scores_for(key_block):
        key_heads = key_block.reshape(seq_count, key_block.shape[1], local_heads, HD)
        raw_scores = (
            jnp.einsum("bqhd,bkhd->bhqk", query_rot, key_heads, preferred_element_type=jnp.float32)
            * score_scale
        )
        return jnp.where(allowed, raw_scores, masked_fill)

    masked = scores_for(keys_all)
    row_max = jnp.max(masked, axis=-1, keepdims=True)
    exponent = jnp.exp(masked - row_max)
    row_total = jnp.sum(exponent, axis=-1, keepdims=True)
    attn_probs = (exponent / row_total).astype(jnp.bfloat16)
    log_total = row_max + jnp.log(row_total)
    value_heads = values_all.reshape(seq_count, values_all.shape[1], local_heads, HD)
    context = jnp.einsum(
        "bhqk,bkhd->bqhd", attn_probs, value_heads, preferred_element_type=jnp.float32
    )
    context = context.reshape(token_count, inner_width).astype(jnp.bfloat16)
    up_proj = project(w_up, up_bias)
    activated = gelu_tanh(up_proj).astype(jnp.bfloat16)
    partial_out = jnp.dot(context, w_out.T, preferred_element_type=jnp.float32) + jnp.dot(
        activated, w_down.T, preferred_element_type=jnp.float32
    )
    branches = lax.psum(partial_out, "tp")
    output = inputs + branches + out_bias.astype(jnp.float32) + down_bias.astype(jnp.float32)
    output = output.astype(jnp.bfloat16).reshape(seq_count, local_rows, model_width)
    back_query, back_key, back_value, back_out, back_up, back_down = (
        lax.all_gather(query_weight, "fsdp", axis=0, tiled=True),
        lax.all_gather(key_weight, "fsdp", axis=0, tiled=True),
        lax.all_gather(value_weight, "fsdp", axis=0, tiled=True),
        lax.all_gather(out_weight, "fsdp", axis=0, tiled=True),
        lax.all_gather(up_weight, "fsdp", axis=0, tiled=True),
        lax.all_gather(down_weight, "fsdp", axis=0, tiled=True),
    )
    keys_back, values_back = (
        lax.all_gather(key_rot, "ctx", axis=1, tiled=True),
        lax.all_gather(value_rows, "ctx", axis=1, tiled=True),
    )
    grad_out = cotangent.reshape(token_count, model_width)
    grad_context = jnp.dot(grad_out, back_out, preferred_element_type=jnp.float32).astype(
        jnp.bfloat16
    )
    grad_heads = grad_context.reshape(seq_count, local_rows, local_heads, HD)
    key_heads_back = keys_back.reshape(seq_count, keys_back.shape[1], local_heads, HD)
    value_heads_back = values_back.reshape(seq_count, values_back.shape[1], local_heads, HD)
    probs_back = jnp.exp(scores_for(keys_back) - log_total)
    grad_probs = jnp.einsum(
        "bqhd,bkhd->bhqk", grad_heads, value_heads_back, preferred_element_type=jnp.float32
    )
    row_delta = jnp.sum(probs_back * grad_probs, axis=-1, keepdims=True)
    grad_scores = (probs_back * (grad_probs - row_delta)).astype(jnp.bfloat16)
    probs_low = probs_back.astype(jnp.bfloat16)
    grad_query_rot = (
        jnp.einsum(
            "bhqk,bkhd->bqhd", grad_scores, key_heads_back, preferred_element_type=jnp.float32
        )
        * score_scale
    )
    row_count = local_rows * lax.axis_size("ctx")
    grad_key_part = (
        jnp.einsum("bhqk,bqhd->kbhd", grad_scores, query_rot, preferred_element_type=jnp.float32)
        * score_scale
    )
    grad_value_part = jnp.einsum(
        "bhqk,bqhd->kbhd", probs_low, grad_heads, preferred_element_type=jnp.float32
    )
    key_grads = lax.psum_scatter(
        jnp.concatenate(
            [
                grad_key_part.reshape(row_count, seq_count, inner_width),
                grad_value_part.reshape(row_count, seq_count, inner_width),
            ],
            axis=2,
        ),
        "ctx",
        scatter_dimension=0,
        tiled=True,
    )
    key_grads = jnp.transpose(key_grads, (1, 0, 2))
    key_grad_rot = key_grads[:, :, :inner_width].reshape(seq_count, local_rows, local_heads, HD)
    grad_value = (
        key_grads[:, :, inner_width:].astype(jnp.bfloat16).reshape(token_count, inner_width)
    )
    grad_query = (
        rotate(grad_query_rot, cosine, -sine_vals)
        .astype(jnp.bfloat16)
        .reshape(token_count, inner_width)
    )
    grad_key = (
        rotate(key_grad_rot, cosine, -sine_vals)
        .astype(jnp.bfloat16)
        .reshape(token_count, inner_width)
    )
    grad_activated = jnp.dot(grad_out, back_down, preferred_element_type=jnp.float32)
    gelu_pull = jax.vjp(gelu_tanh, up_proj)[1]
    grad_up = gelu_pull(grad_activated)[0].astype(jnp.bfloat16)
    partial_hidden = (
        jnp.dot(grad_query, back_query.T, preferred_element_type=jnp.float32)
        + jnp.dot(grad_key, back_key.T, preferred_element_type=jnp.float32)
        + jnp.dot(grad_value, back_value.T, preferred_element_type=jnp.float32)
        + jnp.dot(grad_up, back_up.T, preferred_element_type=jnp.float32)
    )
    grad_hidden = lax.psum(partial_hidden, "tp")
    grad_scaled = grad_hidden * norm_gain
    grad_normed = inv_std * (
        grad_scaled
        - jnp.mean(grad_scaled, axis=-1, keepdims=True)
        - normed * jnp.mean(grad_scaled * normed, axis=-1, keepdims=True)
    )
    grad_float = grad_out.astype(jnp.float32)
    input_grad = (
        (grad_float + grad_normed).astype(jnp.bfloat16).reshape(seq_count, local_rows, model_width)
    )
    small_terms = (
        jnp.sum(grad_hidden * normed, axis=0),
        jnp.sum(grad_hidden, axis=0),
        jnp.sum(grad_query, axis=0, dtype=jnp.float32),
        jnp.sum(grad_key, axis=0, dtype=jnp.float32),
        jnp.sum(grad_value, axis=0, dtype=jnp.float32),
        jnp.sum(grad_up, axis=0, dtype=jnp.float32),
        jnp.sum(grad_float, axis=0),
    )
    gain_grad, shift_grad, qbias_grad, kbias_grad, vbias_grad, ubias_grad, obias_grad = lax.psum(
        (
            small_terms[0],
            small_terms[1],
            small_terms[2],
            small_terms[3],
            small_terms[4],
            small_terms[5],
            small_terms[6],
        ),
        ("fsdp", "ctx"),
    )
    grads_in = jnp.concatenate([grad_query, grad_key, grad_value, grad_up], axis=1)
    acts_out = jnp.concatenate([context, activated], axis=1)
    left_part = jnp.einsum("tc,tn->cn", hidden, grads_in, preferred_element_type=jnp.float32)
    right_part = jnp.einsum("tc,tn->cn", grad_out, acts_out, preferred_element_type=jnp.float32)
    scattered = lax.psum_scatter(
        jnp.concatenate([left_part, right_part], axis=1), "fsdp", scatter_dimension=0, tiled=True
    )
    weight_grads = lax.psum(scattered, "ctx")
    edge_two = 2 * inner_width
    edge_three = 3 * inner_width
    edge_four = edge_three + hidden_units
    edge_five = edge_four + inner_width
    return (
        output,
        input_grad,
        gain_grad,
        shift_grad,
        weight_grads[:, :inner_width],
        qbias_grad,
        weight_grads[:, inner_width:edge_two],
        kbias_grad,
        weight_grads[:, edge_two:edge_three],
        vbias_grad,
        weight_grads[:, edge_four:edge_five],
        weight_grads[:, edge_three:edge_four],
        ubias_grad,
        weight_grads[:, edge_five:],
        obias_grad,
    )


def solution(mesh):
    return jax.shard_map(
        local,
        mesh=mesh,
        in_specs=(
            P("fsdp", "ctx", None),
            P("fsdp", "ctx", None),
            P("fsdp"),
            P(),
            P(),
            P(),
            P("fsdp", "tp"),
            P("tp"),
            P("fsdp", "tp"),
            P("tp"),
            P("fsdp", "tp"),
            P("tp"),
            P("fsdp", "tp"),
            P(),
            P("fsdp", "tp"),
            P("tp"),
            P("fsdp", "tp"),
            P(),
        ),
        out_specs=(
            P("fsdp", "ctx", None),
            P("fsdp", "ctx", None),
            P(),
            P(),
            P("fsdp", "tp"),
            P("tp"),
            P("fsdp", "tp"),
            P("tp"),
            P("fsdp", "tp"),
            P("tp"),
            P("fsdp", "tp"),
            P("fsdp", "tp"),
            P("tp"),
            P("fsdp", "tp"),
            P(),
        ),
        check_vma=False,
    )
```

profile of v0, /device:TPU:0, one launch (start us, length us, event | category | flops | bytes accessed | tf_op | source)
XLA Modules:
  0.0 2836.2 jit_solution(8669938643243681293)
XLA Ops:
  14.0 51.3 %all-gather.9.cloned.1.call-done = bf16[2048,1024]{1,0:T(8,128)(2,1)} async-done(((bf16[512,1024]{1,0:T(8,128)(2,1)}), bf16[2048,1024]{1,0:T(8,128)(2,1)}) %all-gather.9.cloned.1.call-update) | async-done | bytes 4194320 | tf_op jit(solution)/shard_map/all_gather | solution.py:86
  72.7 47.3 %all-gather.15.cloned.1.call-done = bf16[2048,1024]{1,0:T(8,128)(2,1)} async-done(((bf16[512,1024]{1,0:T(8,128)(2,1)}), bf16[2048,1024]{1,0:T(8,128)(2,1)}) %all-gather.15.cloned.1.call-update) | async-done | bytes 4194320 | tf_op jit(solution)/shard_map/all_gather | solution.py:85
  134.8 39.8 %all-gather.13.cloned.1.call-done = bf16[2048,1024]{1,0:T(8,128)(2,1)} async-done(((bf16[512,1024]{1,0:T(8,128)(2,1)}), bf16[2048,1024]{1,0:T(8,128)(2,1)}) %all-gather.13.cloned.1.call-update) | async-done | bytes 4194320 | tf_op jit(solution)/shard_map/all_gather | solution.py:84
  184.9 8.3 fusion.57
  210.7 18.2 all-gather.19.cloned.1.call-done
  242.1 69.7 %all-gather.11.cloned.1.call-done = bf16[2,1024,1024]{2,1,0:T(8,128)(2,1)} async-done(((bf16[2,256,1024]{2,1,0:T(8,128)(2,1)}), bf16[2,1024,1024]{2,1,0:T(8,128)(2,1)}) %all-gather.11.cloned.1.call-update) | async-done | bytes 4194320 | tf_op jit(solution)/shard_map/all_gather | solution.py:126
  318.0 74.9 %all-gather.17.cloned.1.call-done = bf16[2,1024,1024]{1,2,0:T(8,128)(2,1)} async-done(((bf16[2,256,1024]{1,2,0:T(8,128)(2,1)}), bf16[2,1024,1024]{1,2,0:T(8,128)(2,1)}) %all-gather.17.cloned.1.call-update) | async-done | bytes 4194320 | tf_op jit(solution)/shard_map/all_gather | solution.py:125
  392.9 20.1 fusion.59
  412.9 14.6 fusion
  427.5 22.3 multiply_reduce_fusion
  449.8 29.6 %multiply_convert_fusion = bf16[2,16,256,1024]{3,2,1,0:T(8,128)(2,1)} fusion(f32[2,16,256,1024]{3,2,1,0:T(8,128)} %get-tuple-element.72, f32[2,16,256,1024]{3,2,1,0:T(8,128)} %get-tuple-element.70, f32[2,16,256]{2,1,0:T(8,128)S(1)} %get-tuple-element.71, f32[2,16,256]{2,1,0:T(8,128)S(1)} %log_add_fusion), kind=kLoop, calls=%fused_computation.1 | loop fusion | flops 33554432 | bytes 83951616 | tf_op jit(solution)/shard_map/convert_element_type | solution.py:180
  479.4 12.2 broadcast_multiply_fusion
  491.6 17.0 fusion.2
  508.6 11.9 pad_maximum_fusion.1
  521.2 15.1 fusion.43
  539.9 13.7 multiply_bitcast_fusion
  554.9 14.4 fusion.61
  569.3 140.3 %all-gather.23.cloned.1.call-done = bf16[2048,4096]{1,0:T(8,128)(2,1)} async-done(((bf16[512,4096]{1,0:T(8,128)(2,1)}), bf16[2048,4096]{1,0:T(8,128)(2,1)}) %all-gather.23.cloned.1.call-update) | async-done | bytes 16777232 | tf_op jit(solution)/shard_map/all_gather | solution.py:89
  709.6 22.4 convert_reduce_fusion
  732.1 22.1 convolution_bitcast_fusion
  754.2 238.2 %reduce-scatter.3.cloned.1.call-done = f32[256,2,2048]{0,2,1:T(8,128)} async-done(((f32[1024,2,2048]{0,2,1:T(8,128)}), f32[256,2,2048]{0,2,1:T(8,128)}) %reduce-scatter.3.cloned.1.call-update) | async-done | bytes 4194320 | tf_op jit(solution)/shard_map/reduce_scatter | solution.py:196
  1008.6 26.3 fusion.13
  1034.9 65.5 %pad_maximum_fusion = f32[2048,12288]{1,0:T(8,128)} fusion(f32[2048,5120]{1,0:T(8,128)} %convolution_bitcast_fusion, f32[2048,7168]{1,0:T(8,128)} %fusion.13), kind=kLoop, calls=%fused_computation | loop fusion | flops 25165824 | bytes 201326592 | tf_op jit(solution)/shard_map/concatenate | solution.py:269
  1108.4 16.2 convolution_add_fusion
  1137.8 18.3 add_add_fusion
  1156.2 773.7 %reduce-scatter.5.cloned.1.call-done = f32[512,12288]{1,0:T(8,128)} async-done(((f32[2048,12288]{1,0:T(8,128)}), f32[512,12288]{1,0:T(8,128)}) %reduce-scatter.5.cloned.1.call-update) | async-done | bytes 25165840 | tf_op jit(solution)/shard_map/reduce_scatter | solution.py:268
  1932.8 39.2 %all-reduce.7.cloned.1.call-done = (f32[512,2048]{1,0:T(8,128)}, f32[512,2048]{1,0:T(8,128)}) async-done(((f32[512,2048]{1,0:T(8,128)}, f32[512,2048]{1,0:T(8,128)}), (f32[512,2048]{1,0:T(8,128)}, f32[512,2048]{1,0:T(8,128)})) %all-reduce.7.cloned.1.call-update) | async-done | bytes 8388624 | tf_op jit(solution)/shard_map/psum | solution.py:153
  1975.7 82.3 %all-reduce = (f32[2048]{0:T(1024)}, f32[2048]{0:T(1024)}, f32[1024]{0:T(1024)}, f32[1024]{0:T(1024)}, f32[1024]{0:T(1024)}, /*index=5*/f32[4096]{0:T(1024)}, f32[2048]{0:T(1024)}) all-reduce(f32[2048]{0:T(1024)S(1)} %get-tuple-element.15, f32[2048]{0:T(1024)S(1)} %get-tuple-element.18, ...), channel_id=1, replica_groups=mesh['fsdp'=4,'ctx'=4,'tp'=2] {'fsdp','ctx'}, use_global_device_ids=true, to_apply=%region_13.14 | all-reduce | flops 13312 | bytes 106496 | tf_op jit(solution)/shard_map/psum | solution.py:252
  2058.0 6.8 fusion.37
  2064.8 745.8 %all-reduce.5.cloned.1.call-done = f32[512,12288]{1,0:T(8,128)} async-done(((f32[512,12288]{1,0:T(8,128)}), f32[512,12288]{1,0:T(8,128)}) %all-reduce.5.cloned.1.call-update) | async-done | bytes 25165840 | tf_op jit(solution)/shard_map/psum | solution.py:271
  2810.6 7.5 fusion.56
  2818.1 11.1 fusion.55
  (182 shorter events, 125.4 us)
Async XLA Ops:
  7.2 58.1 %all-gather.9.cloned.1.call-start = ((), (), s32[]{:S(2)}) async-start(), calls=%async_computation.2 | async-start | bytes 5242880 | tf_op jit(solution)/shard_map/all_gather | solution.py:86
  8.0 112.0 %all-gather.15.cloned.1.call-start = ((), (), s32[]{:S(2)}) async-start(), calls=%async_computation.5 | async-start | bytes 5242880 | tf_op jit(solution)/shard_map/all_gather | solution.py:85
  8.7 165.8 %all-gather.13.cloned.1.call-start = ((), (), s32[]{:S(2)}) async-start(), calls=%async_computation.4 | async-start | bytes 5242880 | tf_op jit(solution)/shard_map/all_gather | solution.py:84
  9.4 219.5 %all-gather.19.cloned.1.call-start = ((), (), s32[]{:S(2)}) async-start(), calls=%async_computation.7 | async-start | bytes 5242880 | tf_op jit(solution)/shard_map/all_gather | solution.py:87
  10.0 301.7 %all-gather.11.cloned.1.call-start = ((), (), s32[]{:S(2)}) async-start(), calls=%async_computation.3 | async-start | bytes 5242880 | tf_op jit(solution)/shard_map/all_gather | solution.py:126
  14.0 57.7 %copy-start.35 = (bf16[1024]{0:T(1024)(128)(2,1)S(1)}, bf16[1024]{0:T(1024)(128)(2,1)}, u32[]{:S(2)}) copy-start(bf16[1024]{0:T(1024)(128)(2,1)} %param.25) | copy-start | bytes 6148
  14.0 57.8 %copy-start.36 = (bf16[1024]{0:T(1024)(128)(2,1)S(1)}, bf16[1024]{0:T(1024)(128)(2,1)}, u32[]{:S(2)}) copy-start(bf16[1024]{0:T(1024)(128)(2,1)} %param.27) | copy-start | bytes 6148
  14.0 57.8 %copy-start.37 = (s32[8]{0:T(128)S(1)}, s32[8]{0:T(128)}, u32[]{:S(2)}) copy-start(s32[8]{0:T(128)} %param.21) | copy-start | bytes 100
  14.0 105.9 %copy-start.3 = (bf16[512,2048]{1,0:T(8,128)(2,1)S(1)}, bf16[512,2048]{1,0:T(8,128)(2,1)}, u32[]{:S(2)}) copy-start(bf16[512,2048]{1,0:T(8,128)(2,1)} %fusion.32) | copy-start | bytes 6291460
  71.5 321.4 %all-gather.17.cloned.1.call-start = ((), (), s32[]{:S(2)}) async-start(), calls=%async_computation.6 | async-start | bytes 5242880 | tf_op jit(solution)/shard_map/all_gather | solution.py:125
  72.7 128.0 %copy-start.16 = (f32[256,16]{0,1:T(8,128)}, f32[256,16]{0,1:T(8,128)S(1)}, u32[]{:S(2)}) copy-start(f32[256,16]{0,1:T(8,128)S(1)} %get-tuple-element.68) | copy-start | bytes 49156
  204.9 350.0 %all-gather.21.cloned.1.call-start = ((), (), s32[]{:S(2)}) async-start(), calls=%async_computation.8 | async-start | bytes 20971520 | tf_op jit(solution)/shard_map/all_gather | solution.py:88
  205.7 503.9 %all-gather.23.cloned.1.call-start = ((), (), s32[]{:S(2)}) async-start(), calls=%async_computation.9 | async-start | bytes 20971520 | tf_op jit(solution)/shard_map/all_gather | solution.py:89
  206.4 785.9 %reduce-scatter.3.cloned.1.call-start = ((), (), s32[]{:S(2)}) async-start(), calls=%async_computation.10 | async-start | bytes 20971520 | tf_op jit(solution)/shard_map/reduce_scatter | solution.py:196
  242.1 150.8 %copy-start.7 = (bf16[2,256,16,32]{1,3,2,0:T(8,128)(2,1)S(1)}, bf16[2,256,16,32]{1,3,2,0:T(8,128)(2,1)}, u32[]{:S(2)}) copy-start(bf16[2,256,16,32]{1,3,2,0:T(8,128)(2,1)} %copy.99) | copy-start | bytes 1572868
  242.1 150.8 %copy-start.8 = (pred[2,256,1024]{2,1,0:T(8,128)(4,1)S(1)}, pred[2,256,1024]{2,1,0:T(8,128)(4,1)}, u32[]{:S(2)}) copy-start(pred[2,256,1024]{2,1,0:T(8,128)(4,1)} %broadcast_or_fusion) | copy-start | bytes 1572868
  242.1 150.8 %copy-start.14 = (bf16[2,256,16,16]{1,3,2,0:T(8,128)(2,1)S(1)}, bf16[2,256,16,16]{1,3,2,0:T(8,128)(2,1)}, u32[]{:S(2)}) copy-start(bf16[2,256,16,16]{1,3,2,0:T(8,128)(2,1)} %get-tuple-element.57) | copy-start | bytes 786436
  412.9 14.6 copy-start.2
  520.5 1409.4 %reduce-scatter.5.cloned.1.call-start = ((), (), s32[]{:S(2)}) async-start(), calls=%async_computation.11 | async-start | bytes 125829120 | tf_op jit(solution)/shard_map/reduce_scatter | solution.py:268
  539.9 15.0 copy-start.4
  754.1 242.3 %copy-start.17 = (f32[256,16]{0,1:T(8,128)S(1)}, f32[256,16]{0,1:T(8,128)}, u32[]{:S(2)}) copy-start(f32[256,16]{0,1:T(8,128)} %copy-done.16) | copy-start | bytes 49156
  754.1 242.3 %copy-start.20 = (f32[256,16]{0,1:T(8,128)S(1)}, f32[256,16]{0,1:T(8,128)}, u32[]{:S(2)}) copy-start(f32[256,16]{0,1:T(8,128)} %get-tuple-element.66) | copy-start | bytes 49156
  1100.5 871.5 %all-reduce.7.cloned.1.call-start = ((), (), s32[]{:S(2)}) async-start(), calls=%async_computation.13 | async-start | bytes 16777216 | tf_op jit(solution)/shard_map/psum | solution.py:153
  1108.4 16.2 copy-start.12
  1108.4 16.2 copy-start.40
  1156.2 1654.4 %all-reduce.5.cloned.1.call-start = ((), (), s32[]{:S(2)}) async-start(), calls=%async_computation.12 | async-start | bytes 50331648 | tf_op jit(solution)/shard_map/psum | solution.py:271
  1929.9 42.1 %copy-start.1 = (bf16[2,256,2048]{2,1,0:T(8,128)(2,1)S(1)}, bf16[2,256,2048]{2,1,0:T(8,128)(2,1)}, u32[]{:S(2)}) copy-start(bf16[2,256,2048]{2,1,0:T(8,128)(2,1)} %param.18) | copy-start | bytes 6291460
  1929.9 42.1 %copy-start.19 = (f32[2048]{0:T(1024)S(1)}, f32[2048]{0:T(1024)}, u32[]{:S(2)}) copy-start(f32[2048]{0:T(1024)} %copy-done.18) | copy-start | bytes 24580
  1929.9 42.1 %copy-start.22 = (f32[1,2,2,128]{3,1,2,0:T(2,128)S(1)}, f32[1,2,2,128]{3,1,2,0:T(2,128)}, u32[]{:S(2)}) copy-start(f32[1,2,2,128]{3,1,2,0:T(2,128)} %copy-done.21) | copy-start | bytes 6148
  1929.9 42.0 %copy-start.24 = (f32[1,2,2,128]{3,1,2,0:T(2,128)S(1)}, f32[1,2,2,128]{3,1,2,0:T(2,128)}, u32[]{:S(2)}) copy-start(f32[1,2,2,128]{3,1,2,0:T(2,128)} %copy-done.23) | copy-start | bytes 6148
  1930.6 45.0 %copy-start.27 = (f32[4096]{0:T(1024)S(1)}, f32[4096]{0:T(1024)}, u32[]{:S(2)}) copy-start(f32[4096]{0:T(1024)} %get-tuple-element.28) | copy-start | bytes 49156
  1930.6 45.0 %copy-start.28 = (f32[1024]{0:T(1024)S(1)}, f32[1024]{0:T(1024)}, u32[]{:S(2)}) copy-start(f32[1024]{0:T(1024)} %get-tuple-element.30) | copy-start | bytes 12292
  (22 other events, 61.9 us)
Sparse Core Ops, SparseCore 0:
  9.9 55.3 all-gather.8
  67.2 52.6 all-gather.14
  121.8 52.6 all-gather.12
  176.2 52.6 all-gather.18
  230.9 80.7 all-gather.10
  313.7 79.0 all-gather.16
  394.7 155.5 all-gather.20
  552.2 157.4 all-gather.22
  712.0 280.2 reduce-scatter.2
  1100.6 829.2 reduce-scatter.4
  1933.0 38.8 all-reduce.6
  1974.3 836.1 all-reduce.4
where the time goes:
time: 2840 us
  waiting for transfers between devices  2240 us (79%)
  matrix products  263 us (9%)
  other arithmetic  148 us (5%)
  local copies, waits for them, and re-layouts  84.7 us (3%)
  blocking collectives  82.3 us (3%)
    reduce_scatter x1, waiting for transfers between devices, local(): lax.psum_scatter(jnp.concatenate([left_part, right_part], axis=1), 'fsdp'...  774 us
    psum x1, waiting for transfers between devices, local(): weight_grads = lax.psum(scattered, 'ctx')  746 us
    reduce_scatter x1, waiting for transfers between devices, local(): lax.psum_scatter(jnp.concatenate([grad_key_part.reshape(row_count, seq_co...  238 us
    all_gather x1, waiting for transfers between devices, local(): lax.all_gather(down_weight, 'fsdp', axis=0, tiled=True)  140 us
    psum x1, blocking collectives, local(): lax.psum((small_terms[0], small_terms[1], small_terms[2], small_terms[3],...  82.3 us
    all_gather x1, waiting for transfers between devices, local(): lax.all_gather(key_rot, 'ctx', axis=1, tiled=True)  74.9 us
    all_gather x1, waiting for transfers between devices, local(): lax.all_gather(value_rows, 'ctx', axis=1, tiled=True)  69.7 us
    concatenate x1, other arithmetic, local(): jnp.concatenate([left_part, right_part], axis=1)  65.5 us
  transfers between devices with their start and end apart: 12, of which 11 were waited for; matrix products, arithmetic and copies ran while one was open for 13% of the time, Pallas kernels for 0%

commit v1 on v0

--- a/solution.py
+++ b/solution.py
@@ -268,7 +268,11 @@
     scattered = lax.psum_scatter(
         jnp.concatenate([left_part, right_part], axis=1), "fsdp", scatter_dimension=0, tiled=True
     )
-    weight_grads = lax.psum(scattered, "ctx")
+    weight_grads = scattered
+    for hop in (1, 2):
+        weight_grads = weight_grads + lax.ppermute(
+            weight_grads, "ctx", [(dev, dev ^ hop) for dev in range(4)]
+        )
     edge_two = 2 * inner_width
     edge_three = 3 * inner_width
     edge_four = edge_three + hidden_units

time: 2840 us -> 3700 us (1.30)
  blocking collectives: 82.3 us -> 1050 us
  waiting for transfers between devices: 2240 us -> 2090 us
  other arithmetic: 148 us -> 192 us
    psum x1, blocking collectives: 82.3 us -> 1050 us  [local(): lax.psum((small_terms[0], small_terms[1], small_terms[2], small_terms[3],...]
    psum x1 -> x0, waiting for transfers between devices: 746 us -> none  [local(): weight_grads = lax.psum(scattered, 'ctx')]
    ppermute x0 -> x2, waiting for transfers between devices: none -> 540 us  [local(): lax.ppermute(weight_grads, 'ctx', [(dev, dev ^ hop) for dev in range(4)])]
    reduce_scatter x1, waiting for transfers between devices: 774 us -> 829 us  [local(): lax.psum_scatter(jnp.concatenate([left_part, right_part], axis=1), 'fsdp'...]
    add x0 -> x2, other arithmetic: none -> 43.5 us  [local(): weight_grads + lax.ppermute(weight_grads, 'ctx', [(dev, dev ^ hop) for de...]
  transfers between devices with their start and end apart: 12 -> 13, of which waited for: 11 -> 11; matrix products, arithmetic and copies ran while one was open for 13% -> 10% of each run, Pallas kernels for 0% -> 0%
where the time goes in v1:
time: 3700 us; the launch traced here: 3690 us
  waiting for transfers between devices  2090 us (56%)
  blocking collectives  1050 us (28%)
  matrix products  262 us (7%)
  other arithmetic  192 us (5%)
  local copies, waits for them, and re-layouts  83.6 us (2%)
    psum x1, blocking collectives, local(): lax.psum((small_terms[0], small_terms[1], small_terms[2], small_terms[3],...  1050 us
    reduce_scatter x1, waiting for transfers between devices, local(): lax.psum_scatter(jnp.concatenate([left_part, right_part], axis=1), 'fsdp'...  829 us
    ppermute x2, waiting for transfers between devices, local(): lax.ppermute(weight_grads, 'ctx', [(dev, dev ^ hop) for dev in range(4)])  540 us
    reduce_scatter x1, waiting for transfers between devices, local(): lax.psum_scatter(jnp.concatenate([grad_key_part.reshape(row_count, seq_co...  238 us
    all_gather x1, waiting for transfers between devices, local(): lax.all_gather(down_weight, 'fsdp', axis=0, tiled=True)  140 us
    all_gather x1, waiting for transfers between devices, local(): lax.all_gather(key_rot, 'ctx', axis=1, tiled=True)  74.9 us
  transfers between devices with their start and end apart: 13, of which 11 were waited for; matrix products, arithmetic and copies ran while one was open for 10% of the time, Pallas kernels for 0%

profile of v1, /device:TPU:0, one launch (start us, length us, event | category | flops | bytes accessed | tf_op | source)
XLA Modules:
  0.0 3693.7 jit_solution(15389163368561423933)
XLA Ops:
  14.0 51.3 %all-gather.9.cloned.1.call-done = bf16[2048,1024]{1,0:T(8,128)(2,1)} async-done(((bf16[512,1024]{1,0:T(8,128)(2,1)}), bf16[2048,1024]{1,0:T(8,128)(2,1)}) %all-gather.9.cloned.1.call-update) | async-done | bytes 4194320 | tf_op jit(solution)/shard_map/all_gather | solution.py:86
  72.7 47.2 %all-gather.15.cloned.1.call-done = bf16[2048,1024]{1,0:T(8,128)(2,1)} async-done(((bf16[512,1024]{1,0:T(8,128)(2,1)}), bf16[2048,1024]{1,0:T(8,128)(2,1)}) %all-gather.15.cloned.1.call-update) | async-done | bytes 4194320 | tf_op jit(solution)/shard_map/all_gather | solution.py:85
  134.8 39.8 %all-gather.13.cloned.1.call-done = bf16[2048,1024]{1,0:T(8,128)(2,1)} async-done(((bf16[512,1024]{1,0:T(8,128)(2,1)}), bf16[2048,1024]{1,0:T(8,128)(2,1)}) %all-gather.13.cloned.1.call-update) | async-done | bytes 4194320 | tf_op jit(solution)/shard_map/all_gather | solution.py:84
  184.9 8.3 fusion.57
  210.8 18.2 all-gather.19.cloned.1.call-done
  242.1 69.6 %all-gather.11.cloned.1.call-done = bf16[2,1024,1024]{2,1,0:T(8,128)(2,1)} async-done(((bf16[2,256,1024]{2,1,0:T(8,128)(2,1)}), bf16[2,1024,1024]{2,1,0:T(8,128)(2,1)}) %all-gather.11.cloned.1.call-update) | async-done | bytes 4194320 | tf_op jit(solution)/shard_map/all_gather | solution.py:126
  318.0 74.9 %all-gather.17.cloned.1.call-done = bf16[2,1024,1024]{1,2,0:T(8,128)(2,1)} async-done(((bf16[2,256,1024]{1,2,0:T(8,128)(2,1)}), bf16[2,1024,1024]{1,2,0:T(8,128)(2,1)}) %all-gather.17.cloned.1.call-update) | async-done | bytes 4194320 | tf_op jit(solution)/shard_map/all_gather | solution.py:125
  392.9 20.1 fusion.59
  412.9 14.6 fusion
  427.5 22.3 multiply_reduce_fusion
  449.8 29.6 multiply_convert_fusion
  479.4 12.2 broadcast_multiply_fusion
  491.6 17.0 fusion.2
  508.6 11.9 pad_maximum_fusion.1
  521.1 15.1 fusion.43
  539.8 13.7 multiply_bitcast_fusion
  554.9 14.4 fusion.61
  569.3 140.3 %all-gather.23.cloned.1.call-done = bf16[2048,4096]{1,0:T(8,128)(2,1)} async-done(((bf16[512,4096]{1,0:T(8,128)(2,1)}), bf16[2048,4096]{1,0:T(8,128)(2,1)}) %all-gather.23.cloned.1.call-update) | async-done | bytes 16777232 | tf_op jit(solution)/shard_map/all_gather | solution.py:89
  709.6 22.4 convert_reduce_fusion
  732.1 22.1 convolution_bitcast_fusion
  754.2 238.1 %reduce-scatter.3.cloned.1.call-done = f32[256,2,2048]{0,2,1:T(8,128)} async-done(((f32[1024,2,2048]{0,2,1:T(8,128)}), f32[256,2,2048]{0,2,1:T(8,128)}) %reduce-scatter.3.cloned.1.call-update) | async-done | bytes 4194320 | tf_op jit(solution)/shard_map/reduce_scatter | solution.py:196
  1008.6 26.3 fusion.13
  1034.9 65.5 %pad_maximum_fusion = f32[2048,12288]{1,0:T(8,128)} fusion(f32[2048,5120]{1,0:T(8,128)} %convolution_bitcast_fusion, f32[2048,7168]{1,0:T(8,128)} %fusion.13), kind=kLoop, calls=%fused_computation | loop fusion | flops 25165824 | bytes 201326592 | tf_op jit(solution)/shard_map/concatenate | solution.py:269
  1100.5 829.4 %reduce-scatter.5.cloned.1.call-done = f32[512,12288]{1,0:T(8,128)} async-done(((f32[2048,12288]{1,0:T(8,128)}), f32[512,12288]{1,0:T(8,128)}) %reduce-scatter.5.cloned.1.call-update) | async-done | bytes 25165840 | tf_op jit(solution)/shard_map/reduce_scatter | solution.py:268
  1931.3 540.5 %collective-permute-done = f32[512,12288]{1,0:T(8,128)S(1)} collective-permute-done((f32[512,12288]{1,0:T(8,128)}, f32[512,12288]{1,0:T(8,128)S(1)}, u32[]{:S(2)}, u32[]{:S(2)}) %collective-permute-start) | collective-permute-done | bytes 25165856 | tf_op jit(solution)/shard_map/ppermute | solution.py:273
  2471.8 17.7 add.232
  2498.5 15.9 convolution_add_fusion
  2527.6 17.7 add_add_fusion
  2548.1 34.4 all-reduce.4.cloned.1.call-done
  2586.5 1049.2 %all-reduce = (f32[2048]{0:T(1024)}, f32[2048]{0:T(1024)}, f32[1024]{0:T(1024)}, f32[1024]{0:T(1024)}, f32[1024]{0:T(1024)}, /*index=5*/f32[4096]{0:T(1024)}, f32[2048]{0:T(1024)}) all-reduce(f32[2048]{0:T(1024)S(1)} %get-tuple-element.15, f32[2048]{0:T(1024)S(1)} %get-tuple-element.18, ...), channel_id=1, replica_groups=mesh['fsdp'=4,'ctx'=4,'tp'=2] {'fsdp','ctx'}, use_global_device_ids=true, to_apply=%region_13.14 | all-reduce | flops 13312 | bytes 106496 | tf_op jit(solution)/shard_map/psum | solution.py:252
  3642.4 25.8 add.233
  3675.7 11.1 fusion.55
  (185 shorter events, 142.4 us)
Async XLA Ops:
  7.2 58.1 %all-gather.9.cloned.1.call-start = ((), (), s32[]{:S(2)}) async-start(), calls=%async_computation.2 | async-start | bytes 5242880 | tf_op jit(solution)/shard_map/all_gather | solution.py:86
  8.0 112.0 %all-gather.15.cloned.1.call-start = ((), (), s32[]{:S(2)}) async-start(), calls=%async_computation.5 | async-start | bytes 5242880 | tf_op jit(solution)/shard_map/all_gather | solution.py:85
  8.7 165.8 %all-gather.13.cloned.1.call-start = ((), (), s32[]{:S(2)}) async-start(), calls=%async_computation.4 | async-start | bytes 5242880 | tf_op jit(solution)/shard_map/all_gather | solution.py:84
  9.4 219.5 %all-gather.19.cloned.1.call-start = ((), (), s32[]{:S(2)}) async-start(), calls=%async_computation.7 | async-start | bytes 5242880 | tf_op jit(solution)/shard_map/all_gather | solution.py:87
  10.0 301.7 %all-gather.11.cloned.1.call-start = ((), (), s32[]{:S(2)}) async-start(), calls=%async_computation.3 | async-start | bytes 5242880 | tf_op jit(solution)/shard_map/all_gather | solution.py:126
  14.0 57.8 %copy-start.35 = (bf16[1024]{0:T(1024)(128)(2,1)S(1)}, bf16[1024]{0:T(1024)(128)(2,1)}, u32[]{:S(2)}) copy-start(bf16[1024]{0:T(1024)(128)(2,1)} %param.25) | copy-start | bytes 6148
  14.0 57.8 %copy-start.36 = (bf16[1024]{0:T(1024)(128)(2,1)S(1)}, bf16[1024]{0:T(1024)(128)(2,1)}, u32[]{:S(2)}) copy-start(bf16[1024]{0:T(1024)(128)(2,1)} %param.27) | copy-start | bytes 6148
  14.0 57.9 %copy-start.37 = (s32[8]{0:T(128)S(1)}, s32[8]{0:T(128)}, u32[]{:S(2)}) copy-start(s32[8]{0:T(128)} %param.21) | copy-start | bytes 100
  14.0 105.9 %copy-start.3 = (bf16[512,2048]{1,0:T(8,128)(2,1)S(1)}, bf16[512,2048]{1,0:T(8,128)(2,1)}, u32[]{:S(2)}) copy-start(bf16[512,2048]{1,0:T(8,128)(2,1)} %fusion.32) | copy-start | bytes 6291460
  71.5 321.4 %all-gather.17.cloned.1.call-start = ((), (), s32[]{:S(2)}) async-start(), calls=%async_computation.6 | async-start | bytes 5242880 | tf_op jit(solution)/shard_map/all_gather | solution.py:125
  72.7 128.0 %copy-start.16 = (f32[256,16]{0,1:T(8,128)}, f32[256,16]{0,1:T(8,128)S(1)}, u32[]{:S(2)}) copy-start(f32[256,16]{0,1:T(8,128)S(1)} %get-tuple-element.68) | copy-start | bytes 49156
  205.0 349.9 %all-gather.21.cloned.1.call-start = ((), (), s32[]{:S(2)}) async-start(), calls=%async_computation.8 | async-start | bytes 20971520 | tf_op jit(solution)/shard_map/all_gather | solution.py:88
  205.7 503.9 %all-gather.23.cloned.1.call-start = ((), (), s32[]{:S(2)}) async-start(), calls=%async_computation.9 | async-start | bytes 20971520 | tf_op jit(solution)/shard_map/all_gather | solution.py:89
  206.5 785.9 %reduce-scatter.3.cloned.1.call-start = ((), (), s32[]{:S(2)}) async-start(), calls=%async_computation.10 | async-start | bytes 20971520 | tf_op jit(solution)/shard_map/reduce_scatter | solution.py:196
  242.1 150.7 %copy-start.7 = (bf16[2,256,16,32]{1,3,2,0:T(8,128)(2,1)S(1)}, bf16[2,256,16,32]{1,3,2,0:T(8,128)(2,1)}, u32[]{:S(2)}) copy-start(bf16[2,256,16,32]{1,3,2,0:T(8,128)(2,1)} %copy.99) | copy-start | bytes 1572868
  242.1 150.7 %copy-start.8 = (pred[2,256,1024]{2,1,0:T(8,128)(4,1)S(1)}, pred[2,256,1024]{2,1,0:T(8,128)(4,1)}, u32[]{:S(2)}) copy-start(pred[2,256,1024]{2,1,0:T(8,128)(4,1)} %broadcast_or_fusion) | copy-start | bytes 1572868
  242.1 150.7 %copy-start.14 = (bf16[2,256,16,16]{1,3,2,0:T(8,128)(2,1)S(1)}, bf16[2,256,16,16]{1,3,2,0:T(8,128)(2,1)}, u32[]{:S(2)}) copy-start(bf16[2,256,16,16]{1,3,2,0:T(8,128)(2,1)} %get-tuple-element.57) | copy-start | bytes 786436
  520.4 1409.4 %reduce-scatter.5.cloned.1.call-start = ((), (), s32[]{:S(2)}) async-start(), calls=%async_computation.11 | async-start | bytes 125829120 | tf_op jit(solution)/shard_map/reduce_scatter | solution.py:268
  754.2 242.3 %copy-start.17 = (f32[256,16]{0,1:T(8,128)S(1)}, f32[256,16]{0,1:T(8,128)}, u32[]{:S(2)}) copy-start(f32[256,16]{0,1:T(8,128)} %copy-done.16) | copy-start | bytes 49156
  754.2 242.3 %copy-start.20 = (f32[256,16]{0,1:T(8,128)S(1)}, f32[256,16]{0,1:T(8,128)}, u32[]{:S(2)}) copy-start(f32[256,16]{0,1:T(8,128)} %get-tuple-element.66) | copy-start | bytes 49156
  1100.4 1391.5 %copy-start.10 = (bf16[128,8,2,256]{3,1,2,0:T(8,128)(2,1)S(1)}, bf16[128,8,2,256]{3,1,2,0:T(8,128)(2,1)}, u32[]{:S(2)}) copy-start(bf16[128,8,2,256]{3,1,2,0:T(8,128)(2,1)} %copy-done.9) | copy-start | bytes 3145732
  1100.4 1482.1 %all-reduce.4.cloned.1.call-start = ((), (), s32[]{:S(2)}) async-start(), calls=%async_computation.12 | async-start | bytes 16777216 | tf_op jit(solution)/shard_map/psum | solution.py:153
  1929.8 541.9 %collective-permute-start = (f32[512,12288]{1,0:T(8,128)}, f32[512,12288]{1,0:T(8,128)S(1)}, u32[]{:S(2)}, u32[]{:S(2)}) collective-permute-start(f32[512,12288]{1,0:T(8,128)} %reduce-scatter.5.cloned.1.call-done), channel_id=1, source_target_pairs={{0,2},{2,0},{4,6},{6,4},{1,3},{3,1},{5,7},{7,5},{8,10},{10,8},{12,... | collective-permute-start | bytes 75497480 | tf_op jit(solution)/shard_map/ppermute | solution.py:273
  2489.5 1152.9 %collective-permute-start.1 = (f32[512,12288]{1,0:T(8,128)}, f32[512,12288]{1,0:T(8,128)}, u32[]{:S(2)}, u32[]{:S(2)}) collective-permute-start(f32[512,12288]{1,0:T(8,128)} %add.232), channel_id=1, source_target_pairs={{0,4},{2,6},{4,0},{6,2},{1,5},{3,7},{5,1},{7,3},{8,12},{10,14},{12... | collective-permute-start | bytes 75497480 | tf_op jit(solution)/shard_map/ppermute | solution.py:273
  2498.5 15.9 copy-start.12
  2498.5 15.9 copy-start.40
  2545.3 37.3 %copy-start.1 = (bf16[2,256,2048]{2,1,0:T(8,128)(2,1)S(1)}, bf16[2,256,2048]{2,1,0:T(8,128)(2,1)}, u32[]{:S(2)}) copy-start(bf16[2,256,2048]{2,1,0:T(8,128)(2,1)} %param.18) | copy-start | bytes 6291460
  2545.3 37.3 %copy-start.19 = (f32[2048]{0:T(1024)S(1)}, f32[2048]{0:T(1024)}, u32[]{:S(2)}) copy-start(f32[2048]{0:T(1024)} %copy-done.18) | copy-start | bytes 24580
  2545.3 37.2 %copy-start.22 = (f32[1,2,2,128]{3,1,2,0:T(2,128)S(1)}, f32[1,2,2,128]{3,1,2,0:T(2,128)}, u32[]{:S(2)}) copy-start(f32[1,2,2,128]{3,1,2,0:T(2,128)} %copy-done.21) | copy-start | bytes 6148
  2545.3 37.2 %copy-start.24 = (f32[1,2,2,128]{3,1,2,0:T(2,128)S(1)}, f32[1,2,2,128]{3,1,2,0:T(2,128)}, u32[]{:S(2)}) copy-start(f32[1,2,2,128]{3,1,2,0:T(2,128)} %copy-done.23) | copy-start | bytes 6148
  2546.0 40.5 %copy-start.27 = (f32[4096]{0:T(1024)S(1)}, f32[4096]{0:T(1024)}, u32[]{:S(2)}) copy-start(f32[4096]{0:T(1024)} %get-tuple-element.28) | copy-start | bytes 49156
  2546.0 40.5 %copy-start.28 = (f32[1024]{0:T(1024)S(1)}, f32[1024]{0:T(1024)}, u32[]{:S(2)}) copy-start(f32[1024]{0:T(1024)} %get-tuple-element.30) | copy-start | bytes 12292
  (23 other events, 90.2 us)
Sparse Core Ops, SparseCore 0:
  9.9 55.3 all-gather.8
  67.2 52.6 all-gather.14
  121.8 52.6 all-gather.12
  176.2 52.6 all-gather.18
  230.9 80.7 all-gather.10
  313.7 79.0 all-gather.16
  394.7 155.5 all-gather.20
  552.2 157.4 all-gather.22
  712.0 280.2 reduce-scatter.2
  1100.5 829.2 reduce-scatter.4
  2545.5 37.0 all-reduce.3
